TPU v7x, 32 devices: a whole 2x2x4 slice. The times are simulated.
32 devices in a mesh: order: 2 (over core), tok: 16 (over z, y, x).
Axes of the slice: x: 2, y: 2, z: 4, core: 2. Of those that a mesh axis runs over, the one named last changes fastest.
Arguments:
- queries: bfloat16 [65536, 512], P(('order', 'tok')), may hold values from -6 to 6
- key_tokens: bfloat16 [65536, 512], P(('order', 'tok')), may hold values from -6 to 6
- value_tokens: bfloat16 [65536, 512], P(('order', 'tok')), may hold values from -6 to 6
- learn_rates: float32 [65536], P(('order', 'tok')), may hold values from 0.02 to 0.2
- fast_init: float32 [512, 1536], replicated, may hold values from -0.25 to 0.25
- out_gain: float32 [512], replicated, may hold values from 0.5 to 1.5
Outputs:
- output: bfloat16 [65536, 512], P(('order', 'tok'))
All inputs are finite; a program needn't handle non-finite values.
Results may differ from a plain program's by a relative error of at most 0.015.
Values may be sent and summed in bfloat16 or wider, within the bound.
A program may use at most 128 MiB of HBM per device.

v0:
```python
import jax
import jax.numpy as jnp
from jax import lax
from jax.sharding import PartitionSpec as P


def prefix(x, axis, join, neutral):
    place = lax.axis_index(axis)
    gathered = lax.all_gather(x.astype(jnp.bfloat16), axis)
    state = jnp.zeros_like(x) + jnp.asarray(neutral, x.dtype)

    def one(lap, state):
        return join(state, lax.dynamic_index_in_dim(gathered, lap, 0, False).astype(x.dtype))

    return lax.fori_loop(0, place, one, state)


def gate_up(rows_in, weights_bf):
    width = weights_bf.shape[0]
    both_parts = jnp.dot(rows_in, weights_bf[:, : 2 * width], preferred_element_type=jnp.float32)
    return (both_parts[:, :width], both_parts[:, width:])


def backward_terms(key_rows, target, weights_bf):
    width = weights_bf.shape[0]
    gate_pre, up_pre = gate_up(key_rows, weights_bf)
    squash = jax.nn.sigmoid(gate_pre)
    activated = gate_pre * squash
    hidden = (activated * up_pre).astype(jnp.bfloat16)
    hidden_grad = lax.dot_general(
        target,
        weights_bf[:, 2 * width :],
        (((1,), (1,)), ((), ())),
        preferred_element_type=jnp.float32,
    )
    gate_grad = (hidden_grad * up_pre * squash * (1.0 + gate_pre * (1.0 - squash))).astype(
        jnp.bfloat16
    )
    up_grad = (hidden_grad * activated).astype(jnp.bfloat16)
    return (hidden, jnp.concatenate([gate_grad, up_grad], axis=1))


def local_term(key_rows, hidden, inner_grads, target):
    upper = lax.dot_general(
        key_rows, inner_grads, (((0,), (0,)), ((), ())), preferred_element_type=jnp.float32
    )
    lower = lax.dot_general(
        hidden, target, (((0,), (0,)), ((), ())), preferred_element_type=jnp.float32
    )
    return jnp.concatenate([upper, lower], axis=1)


def summed_whole(key_rows, target, weights_bf):
    hidden, inner_grads = backward_terms(key_rows, target, weights_bf)
    return lax.psum(local_term(key_rows, hidden, inner_grads, target), "tok")


def accumulate(earlier, later):
    return earlier + later


def apply_weights(query_rows, weights_bf, out_gain):
    width = weights_bf.shape[0]
    gate_pre, up_pre = gate_up(query_rows, weights_bf)
    hidden = (jax.nn.silu(gate_pre) * up_pre).astype(jnp.bfloat16)
    result = jnp.dot(hidden, weights_bf[:, 2 * width :], preferred_element_type=jnp.float32)
    norm_inv = lax.rsqrt(jnp.mean(result * result, axis=1, keepdims=True) + 1e-06)
    return (result * norm_inv * out_gain[None, :]).astype(jnp.bfloat16)


def shards(queries, key_tokens, value_tokens, learn_rates, fast_init, out_gain):
    group_rows = key_tokens.shape[0] * lax.axis_size("tok")
    factor = group_rows ** (-0.5)
    target = (-(learn_rates[:, None] * factor) * value_tokens.astype(jnp.float32)).astype(
        jnp.bfloat16
    )
    first_step = fast_init - summed_whole(key_tokens, target, fast_init.astype(jnp.bfloat16))
    second_step = first_step - summed_whole(key_tokens, target, first_step.astype(jnp.bfloat16))
    change = second_step - fast_init
    earlier = prefix(change, "order", accumulate, jnp.zeros_like(change))
    closing_bf = (fast_init + earlier + change).astype(jnp.bfloat16)
    return apply_weights(queries, closing_bf, out_gain)


def solution(mesh):
    return jax.shard_map(
        shards,
        mesh=mesh,
        in_specs=(
            P(("order", "tok"), None),
            P(("order", "tok"), None),
            P(("order", "tok"), None),
            P(("order", "tok")),
            P(),
            P(),
        ),
        out_specs=P(("order", "tok"), None),
        check_vma=False,
    )
```

profile of v0, /device:TPU:1, one launch (start us, length us, event | category | flops | bytes accessed | tf_op | source)
XLA Modules:
  0.0 383.2 jit_solution(1011616236271366115)
XLA Ops:
  7.4 2.1 convert_element_type.50
  9.5 2.4 fusion.24
  11.9 2.9 multiply_convert_fusion.6
  14.8 2.1 fusion.11
  16.9 2.3 fusion.18
  19.2 2.0 pad_maximum_fusion
  21.5 3.5 copy.10
  25.0 145.2 %all-reduce.3.cloned.1.call-done = f32[512,1536]{0,1:T(8,128)} async-done(((f32[512,1536]{0,1:T(8,128)}), f32[512,1536]{0,1:T(8,128)}) %all-reduce.3.cloned.1.call-update) | async-done | bytes 3145744 | tf_op jit(solution)/shard_map/psum | solution.py:55
  170.2 5.3 %fusion.38 = (bf16[512,1536]{0,1:T(8,128)(2,1)S(1)}, f32[512,1536]{0,1:T(8,128)}) fusion(f32[512,1536]{0,1:T(8,128)} %copy.10, f32[512,1536]{0,1:T(8,128)} %all-reduce.3.cloned.1.call-done), kind=kLoop, calls=%fused_computation.52 | loop fusion | flops 1572864 | bytes 11010048 | tf_op jit(solution)/shard_map/convert_element_type | solution.py:78
  175.5 2.4 convolution_bitcast_fusion.1
  177.9 3.2 multiply_convert_fusion.3
  181.1 2.1 fusion.12
  183.2 2.3 fusion.15
  185.6 2.0 pad_maximum_fusion.1
  187.6 146.1 %all-reduce.5.cloned.1.call-done = f32[512,1536]{0,1:T(8,128)} async-done(((f32[512,1536]{0,1:T(8,128)}), f32[512,1536]{0,1:T(8,128)}) %all-reduce.5.cloned.1.call-update) | async-done | bytes 3145744 | tf_op jit(solution)/shard_map/psum | solution.py:55
  333.7 4.9 %fusion.21 = bf16[512,1536]{0,1:T(8,128)(2,1)} fusion(f32[512,1536]{0,1:T(8,128)S(1)} %copy-done.2, f32[512,1536]{0,1:T(8,128)} %get-tuple-element.42, f32[512,1536]{0,1:T(8,128)} %all-reduce.5.cloned.1.call-done), kind=kLoop, calls=%fused_computation.35 | loop fusion | flops 2359296 | bytes 11010048 | tf_op jit(solution)/shard_map/convert_element_type | solution.py:9
  338.6 12.0 %all-gather.3.cloned.1.call-done = bf16[1024,1536]{0,1:T(8,128)(2,1)} async-done(((bf16[512,1536]{0,1:T(8,128)(2,1)}), bf16[1024,1536]{0,1:T(8,128)(2,1)}) %all-gather.3.cloned.1.call-update) | async-done | bytes 3145744 | tf_op jit(solution)/shard_map/all_gather | solution.py:9
  350.6 4.6 %copy.13 = bf16[1024,1536]{1,0:T(8,128)(2,1)} copy(bf16[1024,1536]{0,1:T(8,128)(2,1)} %all-gather.3.cloned.1.call-done) | data formatting | bytes 6291456 | tf_op jit(solution)/shard_map/while | solution.py:15
  355.6 2.5 while.10
  355.7 2.2 convert_add_fusion.2
  358.1 2.4 copy.11
  360.5 6.4 %add_convert_fusion = bf16[512,1536]{0,1:T(8,128)(2,1)S(1)} fusion(f32[512,1536]{0,1:T(8,128)} %copy.10, f32[512,1536]{0,1:T(8,128)} %copy.11, f32[512,1536]{0,1:T(8,128)} %get-tuple-element.42, f32[512,1536]{0,1:T(8,128)} %all-reduce.5.cloned.1.call-done), kind=kLoop, calls=%fused_computation.28 | loop fusion | flops 3932160 | bytes 14155776 | tf_op jit(solution)/shard_map/convert_element_type | solution.py:81
  366.8 2.4 convolution_bitcast_fusion
  372.7 3.9 %copy.12 = bf16[2048,512]{1,0:T(8,128)(2,1)} copy(bf16[2048,512]{0,1:T(8,128)(2,1)} %multiply_convert_fusion) | data formatting | bytes 4194304 | tf_op jit(solution)/shard_map/convert_element_type | solution.py:68
  (25 shorter events, 5.0 us)
Async XLA Ops:
  6.5 2.9 copy-start
  6.5 163.7 %all-reduce.3.cloned.1.call-start = ((), (), s32[]{:S(2)}) async-start(), calls=%async_computation | async-start | bytes 6291456 | tf_op jit(solution)/shard_map/psum | solution.py:55
  9.5 2.5 copy-start.4
  21.2 312.4 %all-reduce.5.cloned.1.call-start = ((), (), s32[]{:S(2)}) async-start(), calls=%async_computation.1 | async-start | bytes 6291456 | tf_op jit(solution)/shard_map/psum | solution.py:55
  175.5 2.4 copy-start.5
  187.5 146.2 %copy-start.2 = (f32[512,1536]{0,1:T(8,128)S(1)}, f32[512,1536]{0,1:T(8,128)}, u32[]{:S(2)}) copy-start(f32[512,1536]{0,1:T(8,128)} %copy.10) | copy-start | bytes 9437188
  187.5 163.1 %all-gather.3.cloned.1.call-start = ((), (), s32[]{:S(2)}) async-start(), calls=%async_computation.2 | async-start | bytes 4718592 | tf_op jit(solution)/shard_map/all_gather | solution.py:9
  360.5 6.4 %copy-start.6 = (bf16[2048,512]{1,0:T(8,128)(2,1)S(1)}, bf16[2048,512]{1,0:T(8,128)(2,1)}, u32[]{:S(2)}) copy-start(bf16[2048,512]{1,0:T(8,128)(2,1)} %param.8) | copy-start | bytes 6291460
  369.2 1.7 copy-start.3
  371.0 5.7 %copy-start.1 = (bf16[2048,512]{1,0:T(8,128)(2,1)S(1)}, bf16[2048,512]{1,0:T(8,128)(2,1)}, u32[]{:S(2)}) copy-start(bf16[2048,512]{1,0:T(8,128)(2,1)} %param.9) | copy-start | bytes 6291460
Sparse Core Ops, SparseCore 0:
  21.4 148.7 all-reduce.2
  187.7 145.9 all-reduce.4
  338.7 11.8 all-gather.2
where the time goes:
time: 383 us
  waiting for transfers between devices  303 us (79%)
  other arithmetic  27.4 us (7%)
  matrix products  23.9 us (6%)
  local copies, waits for them, and re-layouts  14.8 us (4%)
  between operations  13.3 us (3%)
    psum x2, waiting for transfers between devices, summed_whole(): return lax.psum(local_term(key_rows, hidden, inner_grads, target), 'tok')  291 us
    all_gather x1, waiting for transfers between devices, prefix(): gathered = lax.all_gather(x.astype(jnp.bfloat16), axis)  12 us
  transfers between devices with their start and end apart: 3, of which 3 were waited for; matrix products, arithmetic and copies ran while one was open for 1% of the time, Pallas kernels for 0%

commit v1 on v0

--- a/solution.py
+++ b/solution.py
@@ -52,7 +52,7 @@
 
 def summed_whole(key_rows, target, weights_bf):
     hidden, inner_grads = backward_terms(key_rows, target, weights_bf)
-    return lax.psum(local_term(key_rows, hidden, inner_grads, target), "tok")
+    return jnp.sum(lax.all_gather(local_term(key_rows, hidden, inner_grads, target), "tok"), axis=0)
 
 
 def accumulate(earlier, later):

time: 383 us -> 1290 us (3.37)
  waiting for transfers between devices: 303 us -> 1060 us
  local copies, waits for them, and re-layouts: 14.8 us -> 121 us
  other arithmetic: 27.4 us -> 65.4 us
    all_gather x0 -> x2, waiting for transfers between devices: none -> 1050 us  [summed_whole(): lax.all_gather(local_term(key_rows, hidden, inner_grads, target), 'tok')]
    psum x2 -> x0, waiting for transfers between devices: 291 us -> none  [summed_whole(): return lax.psum(local_term(key_rows, hidden, inner_grads, target), 'tok')]
    unnamed x15 -> x19, local copies, waits for them, and re-layouts: 3.55 us -> 107 us
    reduce_sum x0 -> x2, other arithmetic: none -> 36.8 us  [summed_whole(): jnp.sum(lax.all_gather(local_term(key_rows, hidden, inner_grads, target),...]
  transfers between devices with their start and end apart: 3 -> 3, of which waited for: 3 -> 3; matrix products, arithmetic and copies ran while one was open for 1% -> 0% of each run, Pallas kernels for 0% -> 0%
where the time goes in v1:
time: 1290 us
  waiting for transfers between devices  1060 us (82%)
  local copies, waits for them, and re-layouts  121 us (9%)
  other arithmetic  65.4 us (5%)
  matrix products  24.1 us (2%)
  between operations  13.3 us (1%)
    all_gather x2, waiting for transfers between devices, summed_whole(): lax.all_gather(local_term(key_rows, hidden, inner_grads, target), 'tok')  1050 us
    unnamed x19, local copies, waits for them, and re-layouts  107 us
    reduce_sum x2, other arithmetic, summed_whole(): jnp.sum(lax.all_gather(local_term(key_rows, hidden, inner_grads, target),...  36.8 us
  transfers between devices with their start and end apart: 3, of which 3 were waited for; matrix products, arithmetic and copies ran while one was open for 0% of the time, Pallas kernels for 0%

profile of v1, /device:TPU:1, one launch (start us, length us, event | category | flops | bytes accessed | tf_op | source)
XLA Modules:
  0.0 1289.2 jit_solution(4921157280094394612)
XLA Ops:
  9.5 2.4 fusion.24
  11.9 2.9 multiply_convert_fusion.6
  16.9 2.3 fusion.18
  21.4 3.5 copy.11
  25.0 526.0 %all-gather.7.cloned.1.call-done = f32[8192,1536]{0,1:T(8,128)} async-done(((f32[512,1536]{0,1:T(8,128)}), f32[8192,1536]{0,1:T(8,128)}) %all-gather.7.cloned.1.call-update) | async-done | bytes 50331664 | tf_op jit(solution)/shard_map/all_gather | solution.py:55
  551.0 51.8 %copy.15 = f32[192,8,16,512]{3,2,1,0:T(8,128)} copy(f32[192,8,16,512]{3,1,2,0:T(8,128)} %bitcast.29) | data formatting | bytes 100663296
  602.8 18.4 %bitcast_reduce_fusion.1 = f32[512,1536]{0,1:T(8,128)} fusion(f32[192,8,16,512]{3,2,1,0:T(8,128)} %copy.15), kind=kLoop, calls=%fused_computation.2 | loop fusion | flops 11796480 | bytes 53477376 | tf_op jit(solution)/shard_map/reduce_sum | solution.py:55
  621.2 4.3 fusion.38
  625.5 2.4 convolution_bitcast_fusion.1
  627.8 3.4 multiply_convert_fusion.3
  631.3 2.1 fusion.12
  633.4 2.3 fusion.15
  637.8 526.9 %all-gather.9.cloned.1.call-done = f32[8192,1536]{0,1:T(8,128)} async-done(((f32[512,1536]{0,1:T(8,128)}), f32[8192,1536]{0,1:T(8,128)}) %all-gather.9.cloned.1.call-update) | async-done | bytes 50331664 | tf_op jit(solution)/shard_map/all_gather | solution.py:55
  1164.7 51.8 %copy.16 = f32[192,8,16,512]{3,2,1,0:T(8,128)} copy(f32[192,8,16,512]{3,1,2,0:T(8,128)} %bitcast.30) | data formatting | bytes 100663296
  1216.5 18.4 %bitcast_reduce_fusion = f32[512,1536]{0,1:T(8,128)} fusion(f32[192,8,16,512]{3,2,1,0:T(8,128)} %copy.16), kind=kLoop, calls=%fused_computation.1 | loop fusion | flops 11796480 | bytes 53477376 | tf_op jit(solution)/shard_map/reduce_sum | solution.py:55
  1234.9 4.9 fusion.21
  1239.8 11.9 all-gather.11.cloned.1.call-done
  1251.7 4.7 copy.14
  1258.5 4.5 while.10
  1258.5 4.5 convert_add_fusion.2
  1263.0 3.5 copy.12
  1266.6 6.4 add_convert_fusion
  1272.9 2.4 convolution_bitcast_fusion
  1278.8 3.9 copy.13
  (31 shorter events, 14.8 us)
Async XLA Ops:
  6.5 2.9 copy-start
  6.5 544.4 %all-gather.7.cloned.1.call-start = ((), (), s32[]{:S(2)}) async-start(), calls=%async_computation | async-start | bytes 53477376 | tf_op jit(solution)/shard_map/all_gather | solution.py:55
  9.5 2.5 copy-start.5
  21.2 1143.5 %all-gather.9.cloned.1.call-start = ((), (), s32[]{:S(2)}) async-start(), calls=%async_computation.1 | async-start | bytes 53477376 | tf_op jit(solution)/shard_map/all_gather | solution.py:55
  602.8 18.4 %copy-start.2 = (f32[512,1536]{0,1:T(8,128)S(1)}, f32[512,1536]{0,1:T(8,128)}, u32[]{:S(2)}) copy-start(f32[512,1536]{0,1:T(8,128)} %copy.11) | copy-start | bytes 9437188
  625.4 2.4 copy-start.6
  637.7 614.0 %all-gather.11.cloned.1.call-start = ((), (), s32[]{:S(2)}) async-start(), calls=%async_computation.2 | async-start | bytes 4718592 | tf_op jit(solution)/shard_map/all_gather | solution.py:9
  1216.5 18.4 %copy-start.3 = (f32[512,1536]{0,1:T(8,128)S(1)}, f32[512,1536]{0,1:T(8,128)}, u32[]{:S(2)}) copy-start(f32[512,1536]{0,1:T(8,128)} %copy.11) | copy-start | bytes 9437188
  1266.6 6.4 copy-start.7
  1275.3 1.7 copy-start.4
  1277.0 5.7 copy-start.1
Sparse Core Ops, SparseCore 0:
  21.3 529.5 all-gather.6
  637.8 526.8 all-gather.8
  1239.9 11.7 all-gather.10
